TPU v7x, 32 devices: a whole 2x2x4 slice. The times are simulated.
32 devices in a mesh: tm: 8 (over z, x), rows: 4 (over y, core).
Axes of the slice: x: 2, y: 2, z: 4, core: 2. Of those that a mesh axis runs over, the one named last changes fastest.
Arguments:
- drift_blocks: bfloat16 [128, 4, 128, 128], P('rows'), may hold values from -0.1875 to 0.1875
- drift_cols: int32 [128, 4], P('rows'), may hold values from 0 to 127
- control_blocks: bfloat16 [4, 128, 128, 128], P(None, 'rows'), may hold values from -0.1875 to 0.1875
- control_cols: int32 [4, 128], P(None, 'rows'), may hold values from 0 to 127
- controls: float32 [4, 40, 8], P(None, 'tm'), may hold values from -4 to 4
- shooting_states: bfloat16 [8, 8, 16384], P('tm', None, 'rows'), may hold values from -6 to 6
- targets: bfloat16 [40, 8, 16384], P('tm', None, 'rows'), may hold values from -6 to 6
Outputs:
- grad_shooting: float32 [8, 8, 16384], P('tm', None, 'rows')
- grad_controls: float32 [4, 40, 8], P(None, 'tm')
- grad_drift: float32 [128, 65536], P('rows', 'tm')
- grad_control_ops: float32 [4, 128, 16384], P(None, 'rows', 'tm')
Inputs may be any that keep to these rules, and one draw needn't show every extreme that they name: `drift_cols`: block column index of each stored drift block; several stored blocks may share a column. `control_cols`: block column index of each stored control block.
All inputs are finite; a program needn't handle non-finite values.
Results may differ from a plain program's by a relative error of at most 0.02.
Values may be sent and summed in bfloat16 or wider, within the bound.
A program may use at most 128 MiB of HBM per device.

v0:
```python
import jax
import jax.numpy as jnp
from jax import lax
from jax.sharding import PartitionSpec as P

defect_weight = 2.0


def passed_along(value, axis, by):
    count = lax.axis_size(axis)
    pairs = [(i, i + by) for i in range(count) if 0 <= i + by < count]
    return lax.ppermute(value, axis, pairs)


def step_terms(gathered, block_width, drift_blocks, drift_cols, control_blocks, control_cols):
    blocks = gathered.reshape(gathered.shape[0], -1, block_width)
    picked = blocks[:, drift_cols]
    drift_out = jnp.einsum(
        "snki,nkoi->sno", picked, drift_blocks, preferred_element_type=jnp.float32
    )
    control_picked = blocks[:, control_cols]
    control_out = jnp.einsum(
        "sjni,jnoi->sjno", control_picked, control_blocks, preferred_element_type=jnp.float32
    )
    return (picked, drift_out, control_picked, control_out)


def shards(
    drift_blocks, drift_cols, control_blocks, control_cols, controls, shooting_states, targets
):
    block_width = drift_blocks.shape[-1]
    scenarios = shooting_states.shape[1]
    local_rows = shooting_states.shape[2]
    horizon_steps = targets.shape[0]
    group_count = lax.axis_size("tm")
    group_index = lax.axis_index("tm")
    total_blocks = drift_blocks.shape[0] * lax.axis_size("rows")
    lifted_total = local_rows * lax.axis_size("rows")
    operators = (drift_blocks, drift_cols, control_blocks, control_cols)
    first_panel = shooting_states[0]
    panels = [first_panel]
    stored = []
    state_panel = first_panel
    for position in range(horizon_steps):
        gathered = lax.all_gather(state_panel, "rows", axis=1, tiled=True)
        step_parts = step_terms(gathered, block_width, *operators)
        stored.append(step_parts)
        weights = controls[:, position].T[:, :, None, None]
        mixed = step_parts[1] + jnp.sum(weights * step_parts[3], axis=1)
        state_panel = mixed.reshape(scenarios, local_rows).astype(jnp.bfloat16)
        panels.append(state_panel)
    group_end = panels[-1]
    next_start = passed_along(first_panel, "tm", -1)
    prev_end = passed_along(group_end, "tm", 1)
    end_wide = group_end.astype(jnp.float32)
    defect = jnp.where(
        group_index < group_count - 1, next_start.astype(jnp.float32) - end_wide, 0.0
    )
    prev_defect = jnp.where(
        group_index > 0, first_panel.astype(jnp.float32) - prev_end.astype(jnp.float32), 0.0
    )
    adjoint = end_wide - targets[horizon_steps - 1].astype(jnp.float32) - defect_weight * defect
    input_grads = [None] * horizon_steps
    mu_list = []
    picked_list = []
    weighted_list = []
    control_picked_list = []
    for position in reversed(range(horizon_steps)):
        adjoint_half = adjoint.astype(jnp.bfloat16)
        picked, drift_out, control_picked, control_out = stored[position]
        mu_blocks = adjoint_half.reshape(scenarios, -1, block_width)
        mu_wide = mu_blocks.astype(jnp.float32)
        weights = controls[:, position].T[:, :, None, None]
        input_grads[position] = jnp.sum(mu_wide[:, None] * control_out, axis=(2, 3)).T
        weighted = (mu_wide[:, None] * weights).astype(jnp.bfloat16)
        mu_list.append(mu_blocks)
        picked_list.append(picked)
        weighted_list.append(weighted)
        control_picked_list.append(control_picked)
        drift_back = jnp.einsum(
            "sno,nkoi->snki", mu_blocks, drift_blocks, preferred_element_type=jnp.float32
        )
        control_back = (
            jnp.einsum(
                "sno,jnoi->sjni", mu_blocks, control_blocks, preferred_element_type=jnp.float32
            )
            * weights
        )
        spread = jnp.zeros((scenarios, total_blocks, block_width), jnp.float32)
        spread = spread.at[:, drift_cols].add(drift_back).at[:, control_cols].add(control_back)
        adjoint = lax.psum_scatter(
            spread.reshape(scenarios, -1).astype(jnp.bfloat16),
            "rows",
            scatter_dimension=1,
            tiled=True,
        ).astype(jnp.float32)
        if position > 0:
            adjoint = (
                adjoint
                + panels[position].astype(jnp.float32)
                - targets[position - 1].astype(jnp.float32)
            )
    all_mu = jnp.concatenate(mu_list, 0)
    all_picked = jnp.concatenate(picked_list, 0)
    drift_sum = jnp.einsum("sno,snki->nkoi", all_mu, all_picked, preferred_element_type=jnp.float32)
    all_weighted = jnp.concatenate(weighted_list, 0)
    all_control_picked = jnp.concatenate(control_picked_list, 0)
    control_sum = jnp.einsum(
        "sjno,sjni->jnoi", all_weighted, all_control_picked, preferred_element_type=jnp.float32
    )
    grad_shooting = (adjoint + defect_weight * prev_defect)[None]
    grad_controls = lax.psum(jnp.stack(input_grads, 1), "rows") * lifted_total ** (-0.5)
    grad_scale = (scenarios * horizon_steps * group_count) ** (-0.5)
    drift_flat = drift_sum.reshape(drift_sum.shape[0], -1)
    grad_drift = lax.psum_scatter(drift_flat, "tm", scatter_dimension=1, tiled=True) * grad_scale
    control_flat = control_sum.reshape(control_sum.shape[0], control_sum.shape[1], -1)
    grad_control_ops = (
        lax.psum_scatter(control_flat, "tm", scatter_dimension=2, tiled=True) * grad_scale
    )
    return (grad_shooting, grad_controls, grad_drift, grad_control_ops)


def solution(mesh):
    return jax.shard_map(
        shards,
        mesh=mesh,
        in_specs=(
            P("rows", None, None, None),
            P("rows", None),
            P(None, "rows", None, None),
            P(None, "rows"),
            P(None, "tm", None),
            P("tm", None, "rows"),
            P("tm", None, "rows"),
        ),
        out_specs=(
            P("tm", None, "rows"),
            P(None, "tm", None),
            P("rows", "tm"),
            P(None, "rows", "tm"),
        ),
        check_vma=False,
    )
```

profile of v0, /device:TPU:0, one launch (start us, length us, event | category | flops | bytes accessed | tf_op | source)
XLA Modules:
  0.0 620.4 jit_solution(2013814788095667245)
XLA Ops:
  8.5 7.5 %all-gather = bf16[1,8,16384]{2,1,0:T(8,128)(2,1)S(1)} all-gather(bf16[1,8,4096]{2,1,0:T(8,128)(2,1)} %param.12), channel_id=2, replica_groups=mesh['tm'=8,'rows'=4] {'rows'}, dimensions={2}, use_global_device_ids=true | all-gather | bytes 327680 | tf_op jit(solution)/shard_map/all_gather | solution.py:45
  19.8 5.4 multiply_reduce_fusion.9
  26.4 5.9 all_gather.16
  33.7 5.4 multiply_reduce_fusion.8
  40.3 5.9 all_gather.17
  47.5 5.4 multiply_reduce_fusion.7
  54.1 5.9 all_gather.18
  61.4 5.4 multiply_reduce_fusion.6
  68.0 6.0 all_gather.19
  74.7 5.3 multiply_reduce_fusion.5
  80.8 4.2 bitcast_dynamic-update-slice_fusion.4
  85.7 1.5 fusion.82
  88.0 9.5 %scatter_fusion = f32[8,128,128]{2,0,1:T(8,128)S(1)} fusion(f32[8,128,128]{2,0,1:T(8,128)S(1)} %broadcast.28.clone, s32[128]{0:T(128)S(1)} %reshape.267, f32[128,8,128]{2,1,0:T(8,128)} %bitcast.344), kind=kCustom, calls=%fused_computation.10 | custom fusion | flops 131072 | bytes 1573376 | tf_op jit(solution)/shard_map/scatter-add | solution.py:90
  97.5 9.5 %scatter_fusion.1 = f32[8,128,128]{2,0,1:T(8,128)S(1)} fusion(f32[8,128,128]{2,0,1:T(8,128)S(1)} %scatter_fusion, s32[128]{0:T(128)S(1)} %reshape.131, f32[128,8,128]{2,1,0:T(8,128)} %bitcast.349), kind=kCustom, calls=%fused_computation.11 | custom fusion | flops 131072 | bytes 1573376 | tf_op jit(solution)/shard_map/scatter-add | solution.py:90
  108.1 22.3 %reduce-scatter.8.cloned.1.call-done = bf16[8,4096]{1,0:T(8,128)(2,1)} async-done(((bf16[8,16384]{1,0:T(8,128)(2,1)}), bf16[8,4096]{1,0:T(8,128)(2,1)}) %reduce-scatter.8.cloned.1.call-update) | async-done | bytes 65552 | tf_op jit(solution)/shard_map/reduce_scatter | solution.py:91
  130.4 1.7 bitcast_dynamic-update-slice_fusion.3
  132.1 2.9 fusion.19
  135.7 4.9 scatter_fusion.2
  140.6 4.9 scatter_fusion.3
  148.0 18.5 %reduce-scatter.10.cloned.1.call-done = bf16[8,4096]{1,0:T(8,128)(2,1)} async-done(((bf16[8,16384]{1,0:T(8,128)(2,1)}), bf16[8,4096]{1,0:T(8,128)(2,1)}) %reduce-scatter.10.cloned.1.call-update) | async-done | bytes 65552 | tf_op jit(solution)/shard_map/reduce_scatter | solution.py:91
  166.6 1.7 bitcast_dynamic-update-slice_fusion.2
  168.3 2.9 fusion.25
  171.2 1.5 fusion.76
  173.5 9.5 %scatter_fusion.4 = f32[8,128,128]{2,0,1:T(8,128)S(1)} fusion(f32[8,128,128]{2,0,1:T(8,128)S(1)} %broadcast.28.clone.2, s32[128]{0:T(128)S(1)} %reshape.267, f32[128,8,128]{2,1,0:T(8,128)} %bitcast.346), kind=kCustom, calls=%fused_computation.14 | custom fusion | flops 131072 | bytes 1573376 | tf_op jit(solution)/shard_map/scatter-add | solution.py:90
  183.0 9.5 %scatter_fusion.5 = f32[8,128,128]{2,0,1:T(8,128)S(1)} fusion(f32[8,128,128]{2,0,1:T(8,128)S(1)} %scatter_fusion.4, s32[128]{0:T(128)S(1)} %reshape.131, f32[128,8,128]{2,1,0:T(8,128)} %bitcast.351), kind=kCustom, calls=%fused_computation.15 | custom fusion | flops 131072 | bytes 1573376 | tf_op jit(solution)/shard_map/scatter-add | solution.py:90
  195.0 1.5 bitcast_convert_fusion.2
  196.4 17.0 %reduce-scatter.12.cloned.1.call-done = bf16[8,4096]{1,0:T(8,128)(2,1)} async-done(((bf16[8,16384]{1,0:T(8,128)(2,1)}), bf16[8,4096]{1,0:T(8,128)(2,1)}) %reduce-scatter.12.cloned.1.call-update) | async-done | bytes 65552 | tf_op jit(solution)/shard_map/reduce_scatter | solution.py:91
  213.5 1.7 bitcast_dynamic-update-slice_fusion.1
  215.2 2.9 fusion.31
  220.4 9.5 %scatter_fusion.6 = f32[8,128,128]{2,0,1:T(8,128)S(1)} fusion(f32[8,128,128]{2,0,1:T(8,128)S(1)} %broadcast.28.clone.3, s32[128]{0:T(128)S(1)} %reshape.267, f32[128,8,128]{2,1,0:T(8,128)} %bitcast.347), kind=kCustom, calls=%fused_computation.16 | custom fusion | flops 131072 | bytes 1573376 | tf_op jit(solution)/shard_map/scatter-add | solution.py:90
  229.9 9.5 %scatter_fusion.7 = f32[8,128,128]{2,0,1:T(8,128)S(1)} fusion(f32[8,128,128]{2,0,1:T(8,128)S(1)} %scatter_fusion.6, s32[128]{0:T(128)S(1)} %reshape.131, f32[128,8,128]{2,1,0:T(8,128)} %bitcast.352), kind=kCustom, calls=%fused_computation.17 | custom fusion | flops 131072 | bytes 1573376 | tf_op jit(solution)/shard_map/scatter-add | solution.py:90
  242.5 17.9 %reduce-scatter.14.cloned.1.call-done = bf16[8,4096]{1,0:T(8,128)(2,1)} async-done(((bf16[8,16384]{1,0:T(8,128)(2,1)}), bf16[8,4096]{1,0:T(8,128)(2,1)}) %reduce-scatter.14.cloned.1.call-update) | async-done | bytes 65552 | tf_op jit(solution)/shard_map/reduce_scatter | solution.py:91
  260.4 1.7 bitcast_dynamic-update-slice_fusion
  262.8 2.8 fusion.37
  267.9 9.5 %scatter_fusion.8 = f32[8,128,128]{2,0,1:T(8,128)S(1)} fusion(f32[8,128,128]{2,0,1:T(8,128)S(1)} %broadcast.28, s32[128]{0:T(128)S(1)} %reshape.267, f32[128,8,128]{2,1,0:T(8,128)} %bitcast.343), kind=kCustom, calls=%fused_computation.18 | custom fusion | flops 131072 | bytes 1573376 | tf_op jit(solution)/shard_map/scatter-add | solution.py:90
  277.4 9.5 %scatter_fusion.9 = f32[8,128,128]{2,0,1:T(8,128)S(1)} fusion(f32[8,128,128]{2,0,1:T(8,128)S(1)} %scatter_fusion.8, s32[128]{0:T(128)S(1)} %reshape.131, f32[128,8,128]{2,1,0:T(8,128)} %bitcast.348), kind=kCustom, calls=%fused_computation.19 | custom fusion | flops 131072 | bytes 1573376 | tf_op jit(solution)/shard_map/scatter-add | solution.py:90
  288.8 4.5 fusion.89
  293.3 9.4 %reshape.115 = f32[4,32,16384]{2,1,0:T(8,128)} reshape(f32[4,32,128,128]{3,2,1,0:T(8,128)} %fusion.89) | data formatting | bytes 16777216 | tf_op jit(solution)/shard_map/reshape | solution.py:116
  304.1 4.6 convolution_bitcast_fusion
  308.6 9.0 %copy.28 = f32[32,4,128,128]{3,2,1,0:T(8,128)} copy(f32[32,4,128,128]{2,3,1,0:T(8,128)} %convolution_bitcast_fusion) | data formatting | bytes 16777216 | tf_op jit(solution)/shard_map/sno,snki->nkoi/transpose | solution.py:105
  317.6 12.2 %copy.72 = f32[4,8,512,128]{3,1,2,0:T(8,128)} copy(f32[4,8,512,128]{3,2,1,0:T(8,128)} %bitcast.317) | data formatting | bytes 16777216
  330.6 3.5 collective-permute-start.1
  334.9 10.9 %psum.7 = f32[4,5,8]{2,0,1:T(4,128)S(1)} all-reduce(f32[4,5,8]{2,0,1:T(4,128)S(1)} %constant_dynamic-update-slice_fusion), channel_id=1, replica_groups=mesh['tm'=8,'rows'=4] {'rows'}, use_global_device_ids=true, to_apply=%region_25.26 | all-reduce | flops 160 | bytes 1280 | tf_op jit(solution)/shard_map/psum | solution.py:112
  346.5 1.5 add_bitcast_fusion
  348.0 112.7 %reduce-scatter.20.cloned.1.call-done = f32[4,32,2048]{2,1,0:T(8,128)} async-done(((f32[4,32,16384]{2,1,0:T(8,128)}), f32[4,32,2048]{2,1,0:T(8,128)}) %reduce-scatter.20.cloned.1.call-update) | async-done | bytes 1048592 | tf_op jit(solution)/shard_map/reduce_scatter | solution.py:118
  460.7 2.3 broadcast_multiply_fusion
  463.0 148.3 %reduce-scatter.18.cloned.1.call-done = f32[32,8192]{1,0:T(8,128)} async-done(((f32[32,65536]{1,0:T(8,128)}), f32[32,8192]{1,0:T(8,128)}) %reduce-scatter.18.cloned.1.call-update) | async-done | bytes 1048592 | tf_op jit(solution)/shard_map/reduce_scatter | solution.py:115
  611.3 2.3 broadcast_multiply_fusion.1
  (172 shorter events, 38.3 us)
Async XLA Ops:
  7.2 123.2 %reduce-scatter.8.cloned.1.call-start = ((), (), s32[]{:S(2)}) async-start(), calls=%async_computation.7 | async-start | bytes 327680 | tf_op jit(solution)/shard_map/reduce_scatter | solution.py:91
  7.2 73.6 %collective-permute-start = (bf16[8,4096]{1,0:T(8,128)(2,1)}, bf16[8,4096]{1,0:T(8,128)(2,1)S(1)}, u32[]{:S(2)}, u32[]{:S(2)}) collective-permute-start(bf16[8,4096]{1,0:T(8,128)(2,1)} %bitcast.353), channel_id=1, source_target_pairs={{4,0},{8,4},{12,8},{16,12},{20,16},{24,20},{28,24},{5,1},{9,5},{13... | collective-permute-start | bytes 196616 | tf_op jit(solution)/shard_map/ppermute | solution.py:12
  18.2 29.4 %copy-start.39 = (f32[8,4]{0,1:T(4,128)}, f32[8,4]{0,1:T(4,128)S(1)}, u32[]{:S(2)}) copy-start(f32[8,4]{0,1:T(4,128)S(1)} %get-tuple-element.15) | copy-start | bytes 388
  18.2 66.9 %copy-start.41 = (f32[8,4]{0,1:T(4,128)}, f32[8,4]{0,1:T(4,128)S(1)}, u32[]{:S(2)}) copy-start(f32[8,4]{0,1:T(4,128)S(1)} %get-tuple-element.14) | copy-start | bytes 388
  18.2 113.9 %copy-start.40 = (f32[8,4]{0,1:T(4,128)}, f32[8,4]{0,1:T(4,128)S(1)}, u32[]{:S(2)}) copy-start(f32[8,4]{0,1:T(4,128)S(1)} %get-tuple-element.18) | copy-start | bytes 388
  19.8 5.4 copy-start.1
  26.4 5.9 copy-start.33
  33.6 6.6 %copy-start.10 = (bf16[128,8,128]{2,1,0:T(8,128)(2,1)}, bf16[128,8,128]{2,1,0:T(8,128)(2,1)S(1)}, u32[]{:S(2)}) copy-start(bf16[128,8,128]{2,1,0:T(8,128)(2,1)S(1)} %gather_fusion.2) | copy-start | bytes 786436
  33.7 5.4 copy-start.2
  40.3 5.9 copy-start.34
  47.5 6.6 %copy-start.12 = (bf16[128,8,128]{2,1,0:T(8,128)(2,1)}, bf16[128,8,128]{2,1,0:T(8,128)(2,1)S(1)}, u32[]{:S(2)}) copy-start(bf16[128,8,128]{2,1,0:T(8,128)(2,1)S(1)} %gather_fusion.4) | copy-start | bytes 786436
  47.5 5.4 copy-start.3
  54.1 5.9 copy-start.35
  61.4 6.6 %copy-start.14 = (bf16[128,8,128]{2,1,0:T(8,128)(2,1)}, bf16[128,8,128]{2,1,0:T(8,128)(2,1)S(1)}, u32[]{:S(2)}) copy-start(bf16[128,8,128]{2,1,0:T(8,128)(2,1)S(1)} %gather_fusion.6) | copy-start | bytes 786436
  61.4 5.4 copy-start.4
  80.8 4.9 copy-start.16
  80.8 4.2 copy-start
  80.8 4.9 copy-start.5
  85.0 2.1 copy-start.29
  107.8 58.8 %reduce-scatter.10.cloned.1.call-start = ((), (), s32[]{:S(2)}) async-start(), calls=%async_computation.8 | async-start | bytes 327680 | tf_op jit(solution)/shard_map/reduce_scatter | solution.py:91
  130.4 4.6 copy-start.6
  132.1 2.9 copy-start.30
  146.3 67.1 %reduce-scatter.12.cloned.1.call-start = ((), (), s32[]{:S(2)}) async-start(), calls=%async_computation.9 | async-start | bytes 327680 | tf_op jit(solution)/shard_map/reduce_scatter | solution.py:91
  166.6 4.6 copy-start.7
  168.3 4.3 copy-start.31
  193.2 67.1 %reduce-scatter.14.cloned.1.call-start = ((), (), s32[]{:S(2)}) async-start(), calls=%async_computation.10 | async-start | bytes 327680 | tf_op jit(solution)/shard_map/reduce_scatter | solution.py:91
  194.1 21.0 %copy-start.23 = (f32[8,32,128]{2,0,1:T(8,128)}, f32[8,32,128]{2,0,1:T(8,128)S(1)}, u32[]{:S(2)}) copy-start(f32[8,32,128]{2,0,1:T(8,128)S(1)} %bitcast_convert_fusion.3) | copy-start | bytes 393220
  213.5 4.6 copy-start.8
  215.2 4.3 copy-start.32
  240.1 106.3 %reduce-scatter.16.cloned.1.call-start = ((), (), s32[]{:S(2)}) async-start(), calls=%async_computation.11 | async-start | bytes 327680 | tf_op jit(solution)/shard_map/reduce_scatter | solution.py:91
  242.3 19.8 %copy-start.26 = (f32[8,32,128]{2,0,1:T(8,128)}, f32[8,32,128]{2,0,1:T(8,128)S(1)}, u32[]{:S(2)}) copy-start(f32[8,32,128]{2,0,1:T(8,128)S(1)} %bitcast_convert_fusion.1) | copy-start | bytes 393220
  260.4 5.2 copy-start.9
  287.7 173.0 %reduce-scatter.20.cloned.1.call-start = ((), (), s32[]{:S(2)}) async-start(), calls=%async_computation.13 | async-start | bytes 9437184 | tf_op jit(solution)/shard_map/reduce_scatter | solution.py:118
  302.7 1.1 copy-start.13
  302.7 1.2 copy-start.11
  302.7 1.3 copy-start.36
  302.8 308.5 %reduce-scatter.18.cloned.1.call-start = ((), (), s32[]{:S(2)}) async-start(), calls=%async_computation.12 | async-start | bytes 9437184 | tf_op jit(solution)/shard_map/reduce_scatter | solution.py:115
  329.8 4.4 copy-start.22
  329.8 4.5 copy-start.21
  329.8 4.5 copy-start.24
  329.8 4.7 copy-start.20
  329.8 4.7 copy-start.25
  329.8 4.8 copy-start.19
  329.8 4.8 copy-start.27
  329.8 4.9 copy-start.18
  329.8 4.9 copy-start.28
  329.8 16.6 %copy-start.37 = (bf16[1,8,4096]{2,1,0:T(8,128)(2,1)S(1)}, bf16[1,8,4096]{2,1,0:T(8,128)(2,1)}, u32[]{:S(2)}) copy-start(bf16[1,8,4096]{2,1,0:T(8,128)(2,1)} %param.12) | copy-start | bytes 196612
  330.6 15.9 %collective-permute-start.1 = (bf16[8,4096]{1,0:T(8,128)(2,1)S(1)}, bf16[8,4096]{1,0:T(8,128)(2,1)S(1)}, u32[]{:S(2)}, u32[]{:S(2)}) collective-permute-start(bf16[8,4096]{1,0:T(8,128)(2,1)S(1)} %copy-done.38), channel_id=1, source_target_pairs={{0,4},{4,8},{8,12},{12,16},{16,20},{20,24},{24,28},{1,5},{5,9},{9,... | collective-permute-start | bytes 196616 | tf_op jit(solution)/shard_map/ppermute | solution.py:12
  (3 other events, 2.8 us)
Sparse Core Ops, SparseCore 0:
  107.9 22.4 reduce-scatter.7
  146.4 20.0 reduce-scatter.9
  193.4 20.0 reduce-scatter.11
  240.2 20.0 reduce-scatter.13
  287.8 20.0 reduce-scatter.15
  311.4 149.2 reduce-scatter.19
  464.3 146.9 reduce-scatter.17
where the time goes:
time: 625 us; the launch traced here: 620 us
  waiting for transfers between devices  337 us (54%)
  other arithmetic  114 us (18%)
  matrix products  63.5 us (10%)
  local copies, waits for them, and re-layouts  44.5 us (7%)
  blocking collectives  42 us (7%)
  between operations  14.6 us (2%)
    reduce_scatter x1, waiting for transfers between devices, shards(): lax.psum_scatter(drift_flat, 'tm', scatter_dimension=1, tiled=True)  148 us
    reduce_scatter x1, waiting for transfers between devices, shards(): lax.psum_scatter(control_flat, 'tm', scatter_dimension=2, tiled=True)  113 us
    scatter-add x10, other arithmetic, shards(): spread.at[:, drift_cols].add(drift_back).at[:, control_cols]  85.7 us
    reduce_scatter x5, waiting for transfers between devices, shards(): lax.psum_scatter(spread.reshape(scenarios, -1).astype(jnp.bfloat16), 'row...  75.8 us
    all_gather x5, blocking collectives, shards(): gathered = lax.all_gather(state_panel, 'rows', axis=1, tiled=True)  31.1 us
    dot_general x5, matrix products, step_terms(): jnp.einsum('sjni,jnoi->sjno', control_picked, control_blocks, preferred_e...  27 us
    unnamed x97, local copies, waits for them, and re-layouts  14.5 us
  transfers between devices with their start and end apart: 9, of which 6 were waited for; matrix products, arithmetic and copies ran while one was open for 15% of the time, Pallas kernels for 0%

commit v1 on v0

--- a/solution.py
+++ b/solution.py
@@ -1,6 +1,8 @@
 import jax
 import jax.numpy as jnp
 from jax import lax
+from jax.experimental import pallas as pl
+from jax.experimental.pallas import tpu as pltpu
 from jax.sharding import PartitionSpec as P
 
 defect_weight = 2.0
@@ -25,7 +27,7 @@
     return (picked, drift_out, control_picked, control_out)
 
 
-def shards(
+def general(
     drift_blocks, drift_cols, control_blocks, control_cols, controls, shooting_states, targets
 ):
     block_width = drift_blocks.shape[-1]
@@ -37,6 +39,9 @@
     total_blocks = drift_blocks.shape[0] * lax.axis_size("rows")
     lifted_total = local_rows * lax.axis_size("rows")
     operators = (drift_blocks, drift_cols, control_blocks, control_cols)
+    row_count = lax.axis_size("rows")
+    targets_of = jnp.concatenate([drift_cols.reshape(-1), control_cols.reshape(-1)])
+    hits = (targets_of[:, None] == jnp.arange(total_blocks)[None]).astype(jnp.bfloat16)
     first_panel = shooting_states[0]
     panels = [first_panel]
     stored = []
@@ -86,20 +91,27 @@
             )
             * weights
         )
-        spread = jnp.zeros((scenarios, total_blocks, block_width), jnp.float32)
-        spread = spread.at[:, drift_cols].add(drift_back).at[:, control_cols].add(control_back)
-        adjoint = lax.psum_scatter(
-            spread.reshape(scenarios, -1).astype(jnp.bfloat16),
-            "rows",
-            scatter_dimension=1,
-            tiled=True,
-        ).astype(jnp.float32)
+        terms = jnp.concatenate(
+            [
+                drift_back.reshape(scenarios, -1, block_width),
+                control_back.reshape(scenarios, -1, block_width),
+            ],
+            1,
+        ).astype(jnp.bfloat16)
+        spread = jnp.einsum("gc,sgi->csi", hits, terms, preferred_element_type=jnp.float32)
+        spread = spread.astype(jnp.bfloat16).reshape(row_count, -1, scenarios, block_width)
+        shares = lax.all_to_all(spread, "rows", 0, 0)
+        total = jnp.sum(shares.astype(jnp.float32), 0)
+        adjoint = jnp.swapaxes(total, 0, 1).reshape(scenarios, local_rows)
         if position > 0:
             adjoint = (
                 adjoint
                 + panels[position].astype(jnp.float32)
                 - targets[position - 1].astype(jnp.float32)
             )
+    grad_shooting = (adjoint + defect_weight * prev_defect)[None]
+    grad_controls = lax.psum(jnp.stack(input_grads, 1), "rows") * lifted_total ** (-0.5)
+    grad_scale = (scenarios * horizon_steps * group_count) ** (-0.5)
     all_mu = jnp.concatenate(mu_list, 0)
     all_picked = jnp.concatenate(picked_list, 0)
     drift_sum = jnp.einsum("sno,snki->nkoi", all_mu, all_picked, preferred_element_type=jnp.float32)
@@ -108,9 +120,6 @@
     control_sum = jnp.einsum(
         "sjno,sjni->jnoi", all_weighted, all_control_picked, preferred_element_type=jnp.float32
     )
-    grad_shooting = (adjoint + defect_weight * prev_defect)[None]
-    grad_controls = lax.psum(jnp.stack(input_grads, 1), "rows") * lifted_total ** (-0.5)
-    grad_scale = (scenarios * horizon_steps * group_count) ** (-0.5)
     drift_flat = drift_sum.reshape(drift_sum.shape[0], -1)
     grad_drift = lax.psum_scatter(drift_flat, "tm", scatter_dimension=1, tiled=True) * grad_scale
     control_flat = control_sum.reshape(control_sum.shape[0], control_sum.shape[1], -1)
@@ -118,6 +127,320 @@
         lax.psum_scatter(control_flat, "tm", scatter_dimension=2, tiled=True) * grad_scale
     )
     return (grad_shooting, grad_controls, grad_drift, grad_control_ops)
+
+
+MESH = pl.DeviceIdType.MESH
+F32, BF16 = jnp.float32, jnp.bfloat16
+
+
+def sweep_kernel(
+    dcol, ccol, drift, control, wts, start, nxt, tgt, hits,
+    zall_out, mu_out, lam, last, ig,
+    z0, z1, z2, z3, z4, zfar, muall, bz, terms, spread, outbox, inbox,
+    ag_s, ag_r, zl_s, zl_r, fw_s, fw_r, mu_s, mu_r, rs_s, rs_r, loc,
+):
+    zs = (z0, z1, z2, z3, z4)
+    steps, _, blocks, scen, width = zfar.shape
+    rows = start.shape[0]
+    slots, nu = drift.shape[1], control.shape[0]
+    count = rows * (slots + nu)
+    tm, r = lax.axis_index("tm"), lax.axis_index("rows")
+    q, x = tm // 2, tm % 2
+    peers = range(1, 4)
+
+    def row_peer(d):
+        return {"tm": tm, "rows": r ^ d}
+
+    def line_peer(e):
+        return {"tm": 2 * (q ^ e) + x, "rows": r}
+
+    barrier = pltpu.get_barrier_semaphore()
+    for d in peers:
+        pl.semaphore_signal(barrier, inc=1, device_id=row_peer(d), device_id_type=MESH)
+        pl.semaphore_signal(barrier, inc=1, device_id=line_peer(d), device_id_type=MESH)
+    pl.semaphore_wait(barrier, 6)
+    pending = []
+
+    def send(src, dst, s, t, to):
+        copy = pltpu.make_async_remote_copy(
+            src_ref=src, dst_ref=dst, send_sem=s, recv_sem=t, device_id=to, device_id_type=MESH
+        )
+        copy.start()
+        pending.append(copy)
+        return copy
+
+    def panel(k, row):
+        return zs[k].at[pl.ds(row * rows, rows)]
+
+    def far(k, e, row):
+        return zfar.at[k, e - 1, pl.ds(row * rows, rows)]
+
+    def gather_start(k):
+        return [
+            send(panel(k, r), panel(k, r), ag_s.at[k, d - 1], ag_r.at[k, d - 1], row_peer(d))
+            for d in peers
+        ]
+
+    def line_start(k):
+        return [
+            send(
+                panel(k, r ^ (2 * h)), far(k, e, r ^ (2 * h)),
+                zl_s.at[k, e - 1, h], zl_r.at[k, e - 1, h], line_peer(e),
+            )
+            for e in peers
+            for h in range(2)
+        ]
+
+    def landed_line(k, e, h):
+        there = far(k, e, r ^ (2 * h))
+        return pltpu.make_async_remote_copy(
+            src_ref=there, dst_ref=there, send_sem=zl_s.at[k, e - 1, h],
+            recv_sem=zl_r.at[k, e - 1, h], device_id=line_peer(e), device_id_type=MESH,
+        )
+
+    def pass_on(k):
+        for e in peers:
+            for h in range(2):
+                landed_line(k, e, h).wait_recv()
+                there = far(k, e, r ^ (2 * h))
+                send(there, there, fw_s.at[k, e - 1, h], fw_r.at[k, e - 1, h], row_peer(1))
+
+    zs[0][pl.ds(r * rows, rows)] = start[...]
+    for k in range(steps):
+        for copy in gather_start(k):
+            copy.wait_recv()
+        line_start(k)
+
+        def forward(i, carry):
+            acc = jnp.zeros((scen, width), F32)
+            for m in range(slots):
+                acc += lax.dot_general(
+                    zs[k][dcol[i, m]], drift[i, m], (((1,), (1,)), ((), ())),
+                    preferred_element_type=F32,
+                )
+            for j in range(nu):
+                part = lax.dot_general(
+                    zs[k][ccol[j, i]], control[j, i], (((1,), (1,)), ((), ())),
+                    preferred_element_type=F32,
+                )
+                bz[k, j, i] = part
+                acc += wts[k, j] * part
+            if k + 1 < steps:
+                zs[k + 1][r * rows + i] = acc.astype(BF16)
+            else:
+                last[i] = acc.astype(BF16)
+            return carry
+
+        lax.fori_loop(0, rows, forward, 0, unroll=4)
+    ends = last[...].astype(F32)
+    factor = jnp.where(tm < lax.axis_size("tm") - 1, defect_weight, 0.0)
+    lam[...] = ends - tgt[steps - 1].astype(F32) - factor * (nxt[...].astype(F32) - ends)
+    for k in reversed(range(steps)):
+        muall[k, q] = lam[...].astype(BF16)
+        for e in peers:
+            send(muall.at[k, q], muall.at[k, q], mu_s.at[k, e - 1], mu_r.at[k, e - 1], line_peer(e))
+
+        def backward(i, carry):
+            mu = muall[k, q, i]
+            wide = mu.astype(F32)
+            for m in range(slots):
+                terms[pl.ds(i * slots + m, scen, stride=count), :] = jnp.dot(
+                    mu, drift[i, m], preferred_element_type=F32
+                )
+            sums = []
+            for j in range(nu):
+                sums.append(carry[j] + wide * bz[k, j, i])
+                terms[pl.ds(rows * slots + i * nu + j, scen, stride=count), :] = wts[k, j] * jnp.dot(
+                    mu, control[j, i], preferred_element_type=F32
+                )
+            return tuple(sums)
+
+        zero = jnp.zeros((scen, width), F32)
+        sums = lax.fori_loop(0, rows, backward, (zero,) * nu, unroll=4)
+        for j in range(nu):
+            ig[k, j] = sums[j]
+        for s in range(scen):
+            spread[pl.ds(s, blocks, stride=scen), :] = jnp.dot(
+                hits[...], terms[pl.ds(s * count, count), :].astype(BF16),
+                preferred_element_type=F32,
+            )
+
+        def share(row):
+            at = pl.multiple_of(row * (rows * scen), rows * scen)
+            return spread[pl.ds(at, rows * scen), :].reshape(rows, scen, width)
+
+        arriving = []
+        for d in (2, 3, 1):
+            outbox[k, d - 1] = share(r ^ d).astype(BF16)
+            arriving.append(
+                send(outbox.at[k, d - 1], inbox.at[k, d - 1], rs_s.at[k, d - 1], rs_r.at[k, d - 1], row_peer(d))
+            )
+        pass_on(steps - 1 - k)
+        for copy in arriving:
+            copy.wait_recv()
+        total = share(r)
+        for d in peers:
+            total += inbox[k, d - 1].astype(F32)
+        if k > 0:
+            total += zs[k][pl.ds(r * rows, rows)].astype(F32) - tgt[k - 1].astype(F32)
+        lam[...] = total
+    for k in range(steps):
+        for e in peers:
+            theirs = muall.at[k, q ^ e]
+            pltpu.make_async_remote_copy(
+                src_ref=theirs, dst_ref=theirs, send_sem=mu_s.at[k, e - 1],
+                recv_sem=mu_r.at[k, e - 1], device_id=line_peer(e), device_id_type=MESH,
+            ).wait_recv()
+            for h in range(2):
+                there = far(k, e, r ^ 1 ^ (2 * h))
+                pltpu.make_async_remote_copy(
+                    src_ref=there, dst_ref=there, send_sem=fw_s.at[k, e - 1, h],
+                    recv_sem=fw_r.at[k, e - 1, h], device_id=row_peer(1), device_id_type=MESH,
+                ).wait_recv()
+    local = [pltpu.make_async_copy(muall, mu_out, loc.at[0, 0])]
+    for k in range(steps):
+        local.append(pltpu.make_async_copy(zs[k], zall_out.at[k, q], loc.at[k + 1, 0]))
+        for e in peers:
+            local.append(
+                pltpu.make_async_copy(zfar.at[k, e - 1], zall_out.at[k, q ^ e], loc.at[k + 1, e])
+            )
+    for copy in local:
+        copy.start()
+    for copy in pending:
+        copy.wait_send()
+    for copy in local:
+        copy.wait()
+
+
+def sums_kernel(dcol, ccol, zall, mu, weighted, drift_out, control_out):
+    i = pl.program_id(0)
+    width = zall.shape[-1]
+
+    def picked(c):
+        return zall[:, :, c].astype(F32).reshape(-1, width).astype(BF16)
+
+    drift_out[0] = jnp.dot(mu[0], picked(dcol[i]), preferred_element_type=F32)
+    span = control_out.shape[2]
+    for j in range(control_out.shape[0]):
+        control_out[j, 0] = jnp.dot(
+            weighted[0, j * span : (j + 1) * span, :], picked(ccol[j, i]),
+            preferred_element_type=F32,
+        )
+
+
+def shards(
+    drift_blocks, drift_cols, control_blocks, control_cols, controls, shooting_states, targets
+):
+    group_count, row_count = lax.axis_size("tm"), lax.axis_size("rows")
+    rows, slots, width, _ = drift_blocks.shape
+    nu = control_blocks.shape[0]
+    if not (group_count == 2 * slots and slots == 4 and nu == 4 and row_count == 4 and targets.shape[0] == 5):
+        return general(
+            drift_blocks, drift_cols, control_blocks, control_cols, controls, shooting_states,
+            targets,
+        )
+    steps, scen, local = targets.shape
+    blocks = rows * row_count
+    pairs = group_count // 2
+    group_index = lax.axis_index("tm")
+    pair, half = group_index // 2, group_index % 2
+    first = jnp.swapaxes(shooting_states[0].reshape(scen, rows, width), 0, 1)
+    nxt = passed_along(first, "tm", -1)
+    tgt = jnp.swapaxes(targets.reshape(steps, scen, rows, width), 1, 2)
+    wts = jnp.broadcast_to(
+        jnp.swapaxes(controls, 0, 1)[..., None], (steps, nu, scen, width)
+    )
+    owner = jnp.concatenate([drift_cols.reshape(-1), control_cols.T.reshape(-1)])
+    hits = (jnp.arange(blocks)[:, None] == owner[None]).astype(BF16)
+    count = rows * (slots + nu)
+    vmem = pl.BlockSpec(memory_space=pltpu.VMEM)
+    smem = pl.BlockSpec(memory_space=pltpu.SMEM)
+    hbm = pl.BlockSpec(memory_space=pl.ANY)
+    dma = pltpu.SemaphoreType.DMA
+    zshape = (steps, pairs, blocks, scen, width)
+    mshape = (steps, pairs, rows, scen, width)
+    zall, muall, lam, last, ig = pl.pallas_call(
+        sweep_kernel,
+        out_shape=(
+            jax.ShapeDtypeStruct(zshape, BF16),
+            jax.ShapeDtypeStruct(mshape, BF16),
+            jax.ShapeDtypeStruct((rows, scen, width), F32),
+            jax.ShapeDtypeStruct((rows, scen, width), BF16),
+            jax.ShapeDtypeStruct((steps, nu, scen, width), F32),
+        ),
+        in_specs=[smem, smem] + [vmem] * 7,
+        out_specs=(hbm, hbm, vmem, vmem, vmem),
+        scratch_shapes=[
+            *[pltpu.VMEM((blocks, scen, width), BF16) for _ in range(5)],
+            pltpu.VMEM((steps, pairs - 1, blocks, scen, width), BF16),
+            pltpu.VMEM(mshape, BF16),
+            pltpu.VMEM((steps, nu, rows, scen, width), F32),
+            pltpu.VMEM((scen * count, width), F32),
+            pltpu.VMEM((blocks * scen, width), F32),
+            pltpu.VMEM((steps, 3, rows, scen, width), BF16),
+            pltpu.VMEM((steps, 3, rows, scen, width), BF16),
+            dma((steps, 3)), dma((steps, 3)),
+            dma((steps, 3, 2)), dma((steps, 3, 2)),
+            dma((steps, 3, 2)), dma((steps, 3, 2)),
+            dma((steps, 3)), dma((steps, 3)),
+            dma((steps, 3)), dma((steps, 3)),
+            dma((steps + 1, 4)),
+        ],
+        compiler_params=pltpu.CompilerParams(
+            collective_id=0, has_side_effects=True, vmem_limit_bytes=60 * 2**20
+        ),
+        name="sweep",
+    )(drift_cols, control_cols, drift_blocks, control_blocks, wts, first, nxt, tgt, hits)
+
+    prev_end = passed_along(last, "tm", 1)
+    prev_defect = jnp.where(group_index > 0, first.astype(F32) - prev_end.astype(F32), 0.0)
+    grad_shooting = jnp.swapaxes(lam + defect_weight * prev_defect, 0, 1).reshape(1, scen, local)
+    input_grads = jnp.swapaxes(jnp.sum(ig, -1), 0, 1)
+    grad_controls = lax.psum(input_grads, "rows") * (local * row_count) ** (-0.5)
+    grad_scale = (scen * steps * group_count) ** (-0.5)
+
+    groups = [[i for i in range(group_count) if i % 2 == b] for b in range(2)]
+    inputs = lax.all_gather(controls, "tm", axis_index_groups=groups)
+    span = width // slots
+    depth = steps * pairs * scen
+    cut = lax.dynamic_slice_in_dim(muall, pair * span, span, 4).astype(F32)
+    inputs = inputs.transpose(2, 0, 3, 1)[:, :, None, :, :, None]
+    weighted = (cut[:, :, :, :, None, :] * inputs).astype(BF16)
+    weighted = weighted.transpose(2, 4, 5, 0, 1, 3).reshape(rows, width, depth)
+    mu_t = muall.transpose(2, 4, 0, 1, 3).reshape(rows, width, depth)
+    dcol = lax.dynamic_index_in_dim(drift_cols, pair, 1, keepdims=False)
+    drift_sum, control_sum = pl.pallas_call(
+        sums_kernel,
+        out_shape=(
+            jax.ShapeDtypeStruct((rows, width, width), F32),
+            jax.ShapeDtypeStruct((nu, rows, span, width), F32),
+        ),
+        grid_spec=pltpu.PrefetchScalarGridSpec(
+            num_scalar_prefetch=2,
+            grid=(rows,),
+            in_specs=[
+                pl.BlockSpec(zshape, lambda i, *_: (0, 0, 0, 0, 0), pipeline_mode=pl.Buffered(1)),
+                pl.BlockSpec((1, width, depth), lambda i, *_: (i, 0, 0)),
+                pl.BlockSpec((1, width, depth), lambda i, *_: (i, 0, 0)),
+            ],
+            out_specs=[
+                pl.BlockSpec((1, width, width), lambda i, *_: (i, 0, 0)),
+                pl.BlockSpec((nu, 1, span, width), lambda i, *_: (0, i, 0, 0)),
+            ],
+        ),
+        name="sums",
+    )(dcol, control_cols, zall, mu_t, weighted)
+    drift_two = drift_sum.reshape(rows, 2, -1)
+    control_two = control_sum.reshape(nu, rows, 2, -1)
+    swap = [(i, i ^ 1) for i in range(group_count)]
+
+    def merged(two, axis):
+        mine = lax.dynamic_index_in_dim(two, half, axis, keepdims=False)
+        other = lax.dynamic_index_in_dim(two, 1 - half, axis, keepdims=False)
+        got = lax.ppermute(other.astype(BF16), "tm", swap)
+        return (mine + got.astype(F32)) * grad_scale
+
+    return (grad_shooting, grad_controls, merged(drift_two, 1), merged(control_two, 2))
 
 
 def solution(mesh):

time: 625 us -> 221 us (0.35)
  waiting for transfers between devices: 337 us -> 7.54 us
  Pallas kernels: 0 us -> 125 us
  other arithmetic: 114 us -> 10.9 us
  matrix products: 63.5 us -> 0 us
  blocking collectives: 42 us -> 27.9 us
  between operations: 14.6 us -> 0.84 us
    reduce_scatter x7 -> x0, waiting for transfers between devices: 337 us -> none  [the longest x1 148 us: shards(): lax.psum_scatter(drift_flat, 'tm', scatter_dimension=1, tiled=True)]
    pallas_call x0 -> x2, Pallas kernels: none -> 125 us  [the longest x1 103 us: shards(): pl.pallas_call(sweep_kernel, out_shape=(jax.ShapeDtypeStruct(zshape, BF16...]
    scatter-add x10 -> x0, other arithmetic: 85.7 us -> none  [shards(): spread.at[:, drift_cols].add(drift_back).at[:, control_cols]]
    dot_general x22 -> x0, matrix products: 63.5 us -> none  [the longest x5 27 us: step_terms(): jnp.einsum('sjni,jnoi->sjno', control_picked, control_blocks, preferred_e...]
    mul x5 -> x8, local copies, waits for them, and re-layouts: 3.42 us -> 18.1 us  [shards(): weighted = (cut[:, :, :, :, None, :] * inputs).astype(BF16)]
    all_gather x5 -> x1, blocking collectives: 31.1 us -> 16.8 us  [shards(): inputs = lax.all_gather(controls, 'tm', axis_index_groups=groups)]
    unnamed x97 -> x18, local copies, waits for them, and re-layouts: 14.5 us -> 3.95 us
    unnamed x7 -> x0, other arithmetic: 7.84 us -> none
  transfers between devices with their start and end apart: 9 -> 4, of which waited for: 6 -> 1; matrix products, arithmetic and copies ran while one was open for 15% -> 4% of each run, Pallas kernels for 0% -> 0%
where the time goes in v1:
time: 221 us; the launch traced here: 219 us
  Pallas kernels  125 us (57%)
  local copies, waits for them, and re-layouts  41.3 us (19%)
  blocking collectives  27.9 us (13%)
  other arithmetic  10.9 us (5%)
  waiting for transfers between devices  7.54 us (3%)
  starting transfers between devices  5.86 us (3%)
    pallas_call x1, Pallas kernels, shards(): pl.pallas_call(sweep_kernel, out_shape=(jax.ShapeDtypeStruct(zshape, BF16...  103 us
    pallas_call x1, Pallas kernels, shards(): pl.pallas_call(sums_kernel, out_shape=(jax.ShapeDtypeStruct((rows, width,...  21.9 us
    mul x8, local copies, waits for them, and re-layouts, shards(): weighted = (cut[:, :, :, :, None, :] * inputs).astype(BF16)  18.1 us
    all_gather x1, blocking collectives, shards(): inputs = lax.all_gather(controls, 'tm', axis_index_groups=groups)  16.8 us
    psum x1, blocking collectives, shards(): lax.psum(input_grads, 'rows') * (local * row_count) ** (-0.5)  11 us
    ppermute x2, waiting for transfers between devices, passed_along(): return lax.ppermute(value, axis, pairs)  7.54 us
  transfers between devices with their start and end apart: 4, of which 1 were waited for; matrix products, arithmetic and copies ran while one was open for 4% of the time, Pallas kernels for 0%

profile of v1, /device:TPU:0, one launch (start us, length us, event | category | flops | bytes accessed | tf_op | source)
XLA Modules:
  0.0 219.0 jit_solution(6987687256609170985)
XLA Ops:
  0.6 1.3 collective-permute-start
  2.0 0.8 copy.32.dcol
  2.7 0.1 reshape.39
  2.8 0.8 copy.31
  3.6 0.1 reshape.40
  3.7 0.6 fusion.4.hits
  4.4 0.7 copy.35
  5.1 16.8 %all-gather = f32[16,5,8]{2,1,0:T(8,128)S(1)} all-gather(f32[4,5,8]{2,1,0:T(8,128)S(1)} %copy.35), channel_id=2, replica_groups={{0,8,16,24},{4,12,20,28},{1,9,17,25},{5,13,21,29},{2,10,18,26},{6,14,22..., dimensions={0}, use_global_device_ids=true | all-gather | bytes 3200 | tf_op jit(solution)/shard_map/all_gather | solution.py:403
  21.9 0.2 copy.36
  22.1 0.2 mul.64
  22.3 0.2 mul.65
  22.5 0.1 copy.37
  22.7 1.2 fusion.5.dcol
  23.9 0.0 collective-permute-done.nxt
  23.9 1.4 broadcast_in_dim.5.wts
  25.3 0.0 copy-done.6
  25.3 102.8 %sweep.1 = (bf16[5,4,128,8,128]{4,3,2,1,0:T(8,128)(2,1)}, bf16[5,4,32,8,128]{4,3,2,1,0:T(8,128)(2,1)}, f32[32,8,128]{2,1,0:T(8,128)}, bf16[32,8,128]{2,1,0:T(8,128)(2,1)}, f32[5,4,8,128]{3,2,1,0:T(8,128)}) custom-call(s32[32,4]{1,0:T(8,128)} %copy-done.3, s32[4,32]{1,0:T(4,128)} %ccol.3, bf16[32,4,128,128]{3,2,1,0:T(8,128)(2,1)} %drift.1, ...), custom_call_target="tpu_custom_call" | custom-call | tf_op jit(solution)/shard_map/sweep/pallas_call | solution.py:362
  128.1 1.8 convert_bitcast_fusion
  129.9 0.4 copy.34
  130.2 5.8 %mul.61 = f32[32,4,32,5,4,8]{2,1,5,4,3,0:T(4,128)} broadcast(f32[32,32,5,4,8]{1,4,3,2,0:T(8,128)S(1)} %copy.34), dimensions={0,2,3,4,5} | broadcast | bytes 3276800 | tf_op jit(solution)/shard_map/mul | solution.py:408
  136.0 7.8 %mul.62 = f32[32,128,160]{1,2,0:T(8,128)S(1)} reshape(f32[32,4,32,5,4,8]{2,1,5,4,3,0:T(4,128)} %mul.61) | data formatting | bytes 5242880 | tf_op jit(solution)/shard_map/mul | solution.py:408
  143.8 3.5 %copy.38 = f32[32,128,160]{2,1,0:T(8,128)} copy(f32[32,128,160]{1,2,0:T(8,128)S(1)} %mul.62) | data formatting | bytes 5242880 | tf_op jit(solution)/shard_map/mul | solution.py:408
  147.3 1.5 copy.33
  148.9 2.7 %copy.39.mu = bf16[32,128,160]{2,1,0:T(8,128)(2,1)} copy(bf16[32,128,160]{1,2,0:T(8,128)(2,1)S(1)} %bitcast.44) | data formatting | bytes 2621440 | tf_op jit(solution)/shard_map/reshape | solution.py:410
  151.6 4.0 %multiply_convert_fusion.weighted = bf16[32,128,160]{2,1,0:T(8,128)(2,1)} fusion(f32[32,128,160]{2,1,0:T(8,128)} %copy.38, f32[128,160]{1,0:T(8,128)S(1)} %copy.37), kind=kLoop, calls=%fused_computation | loop fusion | flops 1310720 | bytes 4014080 | tf_op jit(solution)/shard_map/convert_element_type | solution.py:408
  155.6 21.9 %sums.1 = (f32[32,128,128]{2,1,0:T(8,128)}, f32[4,32,32,128]{3,2,1,0:T(8,128)}) custom-call(s32[32]{0:T(128)} %fusion.5.dcol, s32[4,32]{1,0:T(4,128)} %ccol.3, bf16[5,4,128,8,128]{4,3,2,1,0:T(8,128)(2,1)} %get-tuple-element.14.zall, bf16[32,128,160]{2,1,0:T(8,128)(2,1)} %copy.39.mu, bf16[32,128,160]{2,1,0:T(8,128)(2,1)} %multiply_convert_fusion.weighted), custom_call_target="tpu_custom_call" | custom-call | tf_op jit(solution)/shard_map/sums/pallas_call | solution.py:412
  177.5 2.5 %reshape.44 = f32[4,32,2,2048]{3,2,1,0:T(2,128)S(1)} reshape(f32[4,32,32,128]{3,2,1,0:T(8,128)} %get-tuple-element.17) | data formatting | bytes 4194304 | tf_op jit(solution)/shard_map/reshape | solution.py:434
  180.1 1.1 constant_dynamic-slice_fusion
  181.1 2.1 constant_dynamic-slice_fusion.1
  183.2 2.5 %reshape.43 = f32[32,2,8192]{2,1,0:T(2,128)S(1)} reshape(f32[32,128,128]{2,1,0:T(8,128)} %get-tuple-element.16) | data formatting | bytes 4194304 | tf_op jit(solution)/shard_map/reshape | solution.py:433
  185.7 1.1 constant_dynamic-slice_fusion.2
  186.8 2.1 constant_dynamic-slice_fusion.3
  188.9 1.1 copy.55
  190.0 0.6 collective-permute-start.3
  190.6 1.4 copy.54
  192.0 1.4 collective-permute-start.2
  193.4 2.5 %collective-permute-start.1 = (bf16[32,8,128]{2,1,0:T(8,128)(2,1)}, bf16[32,8,128]{2,1,0:T(8,128)(2,1)S(1)}, u32[]{:S(2)}, u32[]{:S(2)}) collective-permute-start(bf16[32,8,128]{2,1,0:T(8,128)(2,1)} %get-tuple-element.12), channel_id=1, source_target_pairs={{0,4},{4,8},{8,12},{12,16},{16,20},{20,24},{24,28},{1,5},{5,9},{9,... | collective-permute-start | bytes 196616 | tf_op jit(solution)/shard_map/ppermute | solution.py:14
  195.9 0.1 reduce_sum.9
  196.1 11.0 %psum.7 = f32[4,5,8]{2,0,1:T(4,128)S(1)} all-reduce(f32[4,5,8]{2,0,1:T(4,128)S(1)} %bitcast.50), channel_id=1, replica_groups=mesh['tm'=8,'rows'=4] {'rows'}, use_global_device_ids=true, to_apply=%region_1.2 | all-reduce | flops 160 | bytes 1280 | tf_op jit(solution)/shard_map/psum | solution.py:399
  207.1 0.6 broadcast_multiply_fusion
  207.7 7.5 %collective-permute-done.1 = bf16[32,8,128]{2,1,0:T(8,128)(2,1)S(1)} collective-permute-done((bf16[32,8,128]{2,1,0:T(8,128)(2,1)}, bf16[32,8,128]{2,1,0:T(8,128)(2,1)S(1)}, u32[]{:S(2)}, u32[]{:S(2)}) %collective-permute-start.1) | collective-permute-done | bytes 65568 | tf_op jit(solution)/shard_map/ppermute | solution.py:14
  215.2 0.0 copy-done.4
  215.2 0.7 add_bitcast_fusion
  215.9 0.0 collective-permute-done.3
  215.9 0.0 copy-done
  215.9 1.5 fusion
  217.4 0.0 collective-permute-done.2
  217.4 1.7 fusion.1
  (12 shorter events, 0.0 us)
Async XLA Ops:
  0.6 23.2 %collective-permute-start = (bf16[32,8,128]{2,1,0:T(8,128)(2,1)}, bf16[32,8,128]{2,1,0:T(8,128)(2,1)S(1)}, u32[]{:S(2)}, u32[]{:S(2)}) collective-permute-start(bf16[32,8,128]{2,1,0:T(8,128)(2,1)} %bitcast.46), channel_id=1, source_target_pairs={{4,0},{8,4},{12,8},{16,12},{20,16},{24,20},{28,24},{5,1},{9,5},{13... | collective-permute-start | bytes 196616 | tf_op jit(solution)/shard_map/ppermute | solution.py:14
  2.7 22.6 %copy-start.3 = (s32[32,4]{1,0:T(8,128)}, s32[32,4]{1,0:T(8,128)S(1)}, u32[]{:S(2)}) copy-start(s32[32,4]{1,0:T(8,128)S(1)} %copy.32.dcol) | copy-start | bytes 1540
  23.9 1.4 copy-start.6
  188.9 7.1 %copy-start.5 = (f32[5,4,8,128]{3,2,1,0:T(8,128)S(1)}, f32[5,4,8,128]{3,2,1,0:T(8,128)}, u32[]{:S(2)}) copy-start(f32[5,4,8,128]{3,2,1,0:T(8,128)} %get-tuple-element.13) | copy-start | bytes 245764
  188.9 26.3 %copy-start.2 = (bf16[1,8,4096]{2,1,0:T(8,128)(2,1)S(1)}, bf16[1,8,4096]{2,1,0:T(8,128)(2,1)}, u32[]{:S(2)}) copy-start(bf16[1,8,4096]{2,1,0:T(8,128)(2,1)} %param.12) | copy-start | bytes 196612
  188.9 26.3 %copy-start.4 = (f32[32,8,128]{2,1,0:T(8,128)S(1)}, f32[32,8,128]{2,1,0:T(8,128)}, u32[]{:S(2)}) copy-start(f32[32,8,128]{2,1,0:T(8,128)} %get-tuple-element.11) | copy-start | bytes 393220
  188.9 27.0 %copy-start = (f32[4,32,1,2048]{3,2,1,0:T(1,128)S(1)}, f32[4,32,1,2048]{3,2,1,0:T(1,128)}, u32[]{:S(2)}) copy-start(f32[4,32,1,2048]{3,2,1,0:T(1,128)} %constant_dynamic-slice_fusion.1) | copy-start | bytes 3145732
  190.0 27.4 %copy-start.1 = (f32[32,1,8192]{2,1,0:T(1,128)S(1)}, f32[32,1,8192]{2,1,0:T(1,128)}, u32[]{:S(2)}) copy-start(f32[32,1,8192]{2,1,0:T(1,128)} %constant_dynamic-slice_fusion.3) | copy-start | bytes 3145732
  190.0 25.9 %collective-permute-start.3 = (bf16[4,32,2048]{2,1,0:T(8,128)(2,1)}, bf16[4,32,2048]{2,1,0:T(8,128)(2,1)S(1)}, u32[]{:S(2)}, u32[]{:S(2)}) collective-permute-start(bf16[4,32,2048]{2,1,0:T(8,128)(2,1)} %bitcast.42), channel_id=1, source_target_pairs={{0,4},{4,0},{8,12},{12,8},{16,20},{20,16},{24,28},{28,24},{1,5},{5... | collective-permute-start | bytes 1572872 | tf_op jit(solution)/shard_map/ppermute | solution.py:440
  192.0 25.4 %collective-permute-start.2 = (bf16[32,8192]{1,0:T(8,128)(2,1)}, bf16[32,8192]{1,0:T(8,128)(2,1)S(1)}, u32[]{:S(2)}, u32[]{:S(2)}) collective-permute-start(bf16[32,8192]{1,0:T(8,128)(2,1)} %bitcast.41), channel_id=1, source_target_pairs={{0,4},{4,0},{8,12},{12,8},{16,20},{20,16},{24,28},{28,24},{1,5},{5... | collective-permute-start | bytes 1572872 | tf_op jit(solution)/shard_map/ppermute | solution.py:440
  193.4 21.8 %collective-permute-start.1 = (bf16[32,8,128]{2,1,0:T(8,128)(2,1)}, bf16[32,8,128]{2,1,0:T(8,128)(2,1)S(1)}, u32[]{:S(2)}, u32[]{:S(2)}) collective-permute-start(bf16[32,8,128]{2,1,0:T(8,128)(2,1)} %get-tuple-element.12), channel_id=1, source_target_pairs={{0,4},{4,8},{8,12},{12,16},{16,20},{20,24},{24,28},{1,5},{5,9},{9,... | collective-permute-start | bytes 196616 | tf_op jit(solution)/shard_map/ppermute | solution.py:14

commit v2 on v1

--- a/solution.py
+++ b/solution.py
@@ -134,13 +134,16 @@
 
 
 def sweep_kernel(
-    dcol, ccol, drift, control, wts, start, nxt, tgt, hits,
-    zall_out, mu_out, lam, last, ig,
+    dcol, ccol, drift, control, wts, wex, start, tgt, hits,
+    gshoot, ig, gdrift, gcontrol,
     z0, z1, z2, z3, z4, zfar, muall, bz, terms, spread, outbox, inbox,
-    ag_s, ag_r, zl_s, zl_r, fw_s, fw_r, mu_s, mu_r, rs_s, rs_r, loc,
+    lam, last, nxt, before, igin, wfar, wall, cut, xd_out, xd_in, xc_out, xc_in,
+    ag_s, ag_r, zl_s, zl_r, fw_s, fw_r, mu_s, mu_r, rs_s, rs_r,
+    ig_s, ig_r, wx_s, wx_r, nb_s, nb_r, xd_s, xd_r, xc_s, xc_r,
 ):
     zs = (z0, z1, z2, z3, z4)
-    steps, _, blocks, scen, width = zfar.shape
+    steps, blocks, scen, width = muall.shape[0], *zfar.shape[2:]
+    pairs = muall.shape[1]
     rows = start.shape[0]
     slots, nu = drift.shape[1], control.shape[0]
     count = rows * (slots + nu)
@@ -158,7 +161,13 @@
     for d in peers:
         pl.semaphore_signal(barrier, inc=1, device_id=row_peer(d), device_id_type=MESH)
         pl.semaphore_signal(barrier, inc=1, device_id=line_peer(d), device_id_type=MESH)
-    pl.semaphore_wait(barrier, 6)
+    group_count = lax.axis_size("tm")
+    side = {"tm": tm ^ 1, "rows": r}
+    after = {"tm": lax.rem(tm + 1, group_count), "rows": r}
+    ahead = {"tm": lax.rem(tm + group_count - 1, group_count), "rows": r}
+    for device in (side, after, ahead):
+        pl.semaphore_signal(barrier, inc=1, device_id=device, device_id_type=MESH)
+    pl.semaphore_wait(barrier, 9)
     pending = []
 
     def send(src, dst, s, t, to):
@@ -206,8 +215,13 @@
                 send(there, there, fw_s.at[k, e - 1, h], fw_r.at[k, e - 1, h], row_peer(1))
 
     zs[0][pl.ds(r * rows, rows)] = start[...]
+    first_step = gather_start(0)
+    from_next = send(start, nxt, nb_s.at[0], nb_r.at[0], ahead)
+    controls_in = [
+        send(wex, wfar.at[e - 1], wx_s.at[e - 1], wx_r.at[e - 1], line_peer(e)) for e in peers
+    ]
     for k in range(steps):
-        for copy in gather_start(k):
+        for copy in first_step if k == 0 else gather_start(k):
             copy.wait_recv()
         line_start(k)
 
@@ -232,16 +246,19 @@
             return carry
 
         lax.fori_loop(0, rows, forward, 0, unroll=4)
+    from_prev = send(last, before, nb_s.at[1], nb_r.at[1], after)
+    from_next.wait_recv()
     ends = last[...].astype(F32)
     factor = jnp.where(tm < lax.axis_size("tm") - 1, defect_weight, 0.0)
     lam[...] = ends - tgt[steps - 1].astype(F32) - factor * (nxt[...].astype(F32) - ends)
+    partial_in = []
     for k in reversed(range(steps)):
-        muall[k, q] = lam[...].astype(BF16)
+        muall[k, 0] = lam[...].astype(BF16)
         for e in peers:
-            send(muall.at[k, q], muall.at[k, q], mu_s.at[k, e - 1], mu_r.at[k, e - 1], line_peer(e))
+            send(muall.at[k, 0], muall.at[k, e], mu_s.at[k, e - 1], mu_r.at[k, e - 1], line_peer(e))
 
         def backward(i, carry):
-            mu = muall[k, q, i]
+            mu = muall[k, 0, i]
             wide = mu.astype(F32)
             for m in range(slots):
                 terms[pl.ds(i * slots + m, scen, stride=count), :] = jnp.dot(
@@ -259,6 +276,10 @@
         sums = lax.fori_loop(0, rows, backward, (zero,) * nu, unroll=4)
         for j in range(nu):
             ig[k, j] = sums[j]
+        for d in peers:
+            partial_in.append(
+                send(ig.at[k], igin.at[k, d - 1], ig_s.at[k, d - 1], ig_r.at[k, d - 1], row_peer(d))
+            )
         for s in range(scen):
             spread[pl.ds(s, blocks, stride=scen), :] = jnp.dot(
                 hits[...], terms[pl.ds(s * count, count), :].astype(BF16),
@@ -286,7 +307,7 @@
         lam[...] = total
     for k in range(steps):
         for e in peers:
-            theirs = muall.at[k, q ^ e]
+            theirs = muall.at[k, e]
             pltpu.make_async_remote_copy(
                 src_ref=theirs, dst_ref=theirs, send_sem=mu_s.at[k, e - 1],
                 recv_sem=mu_r.at[k, e - 1], device_id=line_peer(e), device_id_type=MESH,
@@ -297,35 +318,75 @@
                     src_ref=there, dst_ref=there, send_sem=fw_s.at[k, e - 1, h],
                     recv_sem=fw_r.at[k, e - 1, h], device_id=row_peer(1), device_id_type=MESH,
                 ).wait_recv()
-    local = [pltpu.make_async_copy(muall, mu_out, loc.at[0, 0])]
+    from_prev.wait_recv()
+    back = jnp.where(tm > 0, defect_weight, 0.0)
+    gshoot[...] = lam[...] + back * (start[...].astype(F32) - before[...].astype(F32))
+    for copy in controls_in:
+        copy.wait_recv()
     for k in range(steps):
-        local.append(pltpu.make_async_copy(zs[k], zall_out.at[k, q], loc.at[k + 1, 0]))
-        for e in peers:
-            local.append(
-                pltpu.make_async_copy(zfar.at[k, e - 1], zall_out.at[k, q ^ e], loc.at[k + 1, e])
-            )
-    for copy in local:
-        copy.start()
+        for e in range(pairs):
+            at = (k * pairs + e) * scen
+            wall[at : at + scen, :] = wex[k] if e == 0 else wfar[e - 1, k]
+    span = width // slots
+    rowid = lax.broadcasted_iota(jnp.int32, (width, width), 0)
+    laneid = lax.broadcasted_iota(jnp.int32, (width, width), 1)
+    pick = jnp.where(rowid - span * q == laneid % span, 1.0, 0.0).astype(BF16)
+    scale = (scen * steps * group_count) ** (-0.5)
+    depth = steps * pairs * scen
+
+    def picked(c):
+        parts = []
+        for k in range(steps):
+            parts.append(zs[k][c].astype(F32))
+            for e in range(pairs - 1):
+                parts.append(zfar[k, e, c].astype(F32))
+        return jnp.concatenate(parts, 0).astype(BF16)
+
+    def sums_of(i, carry):
+        mu = muall[:, :, i].astype(F32).reshape(depth, width)
+        low = mu.astype(BF16)
+        weighted = jnp.dot(low, pick, preferred_element_type=F32) * wall[...]
+        mu_t = mu.T.astype(BF16)
+        weighted_t = weighted.T.astype(BF16)
+        cut[0] = jnp.dot(mu_t, picked(dcol[i, q]), preferred_element_type=F32) * scale
+        gdrift[i] = cut[0, pl.ds(x * (width // 2), width // 2)]
+        xd_out[i] = cut[0, pl.ds((1 - x) * (width // 2), width // 2)].astype(BF16)
+        for j in range(nu):
+            cut[1, :span] = (
+                jnp.dot(
+                    weighted_t[j * span : (j + 1) * span], picked(ccol[j, i]),
+                    preferred_element_type=F32,
+                )
+                * scale
+            )
+            gcontrol[j, i] = cut[1, pl.ds(x * (span // 2), span // 2)]
+            xc_out[i, j] = cut[1, pl.ds((1 - x) * (span // 2), span // 2)].astype(BF16)
+        return carry
+
+    crossing = []
+    per = rows // xd_s.shape[0]
+    for g in range(xd_s.shape[0]):
+        lax.fori_loop(g * per, (g + 1) * per, sums_of, 0, unroll=2)
+        part = pl.ds(g * per, per)
+        crossing.append(
+            (
+                send(xd_out.at[part], xd_in.at[part], xd_s.at[g], xd_r.at[g], side),
+                send(xc_out.at[part], xc_in.at[part], xc_s.at[g], xc_r.at[g], side),
+            )
+        )
+    for copy in partial_in:
+        copy.wait()
+    ig[...] += igin[:, 0] + igin[:, 1] + igin[:, 2]
+    for g, (one, two) in enumerate(crossing):
+        one.wait_recv()
+        two.wait_recv()
+        part = pl.ds(g * per, per)
+        gdrift[part] += xd_in[part].astype(F32)
+        for j in range(nu):
+            gcontrol[j, part] += xc_in[part, j].astype(F32)
     for copy in pending:
-        copy.wait_send()
-    for copy in local:
-        copy.wait()
-
-
-def sums_kernel(dcol, ccol, zall, mu, weighted, drift_out, control_out):
-    i = pl.program_id(0)
-    width = zall.shape[-1]
-
-    def picked(c):
-        return zall[:, :, c].astype(F32).reshape(-1, width).astype(BF16)
-
-    drift_out[0] = jnp.dot(mu[0], picked(dcol[i]), preferred_element_type=F32)
-    span = control_out.shape[2]
-    for j in range(control_out.shape[0]):
-        control_out[j, 0] = jnp.dot(
-            weighted[0, j * span : (j + 1) * span, :], picked(ccol[j, i]),
-            preferred_element_type=F32,
-        )
+        if not any(copy is other for other in partial_in):
+            copy.wait_send()
 
 
 def shards(
@@ -342,105 +403,78 @@
     steps, scen, local = targets.shape
     blocks = rows * row_count
     pairs = group_count // 2
-    group_index = lax.axis_index("tm")
-    pair, half = group_index // 2, group_index % 2
     first = jnp.swapaxes(shooting_states[0].reshape(scen, rows, width), 0, 1)
-    nxt = passed_along(first, "tm", -1)
     tgt = jnp.swapaxes(targets.reshape(steps, scen, rows, width), 1, 2)
     wts = jnp.broadcast_to(
         jnp.swapaxes(controls, 0, 1)[..., None], (steps, nu, scen, width)
     )
+    span = width // slots
+    wex = jnp.repeat(controls.transpose(1, 2, 0), span, axis=2)
     owner = jnp.concatenate([drift_cols.reshape(-1), control_cols.T.reshape(-1)])
     hits = (jnp.arange(blocks)[:, None] == owner[None]).astype(BF16)
     count = rows * (slots + nu)
     vmem = pl.BlockSpec(memory_space=pltpu.VMEM)
     smem = pl.BlockSpec(memory_space=pltpu.SMEM)
-    hbm = pl.BlockSpec(memory_space=pl.ANY)
     dma = pltpu.SemaphoreType.DMA
-    zshape = (steps, pairs, blocks, scen, width)
-    mshape = (steps, pairs, rows, scen, width)
-    zall, muall, lam, last, ig = pl.pallas_call(
+    groups = 8
+    panel = (rows, scen, width)
+    gshoot, ig, gdrift, gcontrol = pl.pallas_call(
         sweep_kernel,
         out_shape=(
-            jax.ShapeDtypeStruct(zshape, BF16),
-            jax.ShapeDtypeStruct(mshape, BF16),
-            jax.ShapeDtypeStruct((rows, scen, width), F32),
-            jax.ShapeDtypeStruct((rows, scen, width), BF16),
+            jax.ShapeDtypeStruct(panel, F32),
             jax.ShapeDtypeStruct((steps, nu, scen, width), F32),
+            jax.ShapeDtypeStruct((rows, width // 2, width), F32),
+            jax.ShapeDtypeStruct((nu, rows, span // 2, width), F32),
         ),
         in_specs=[smem, smem] + [vmem] * 7,
-        out_specs=(hbm, hbm, vmem, vmem, vmem),
+        out_specs=(vmem,) * 4,
         scratch_shapes=[
             *[pltpu.VMEM((blocks, scen, width), BF16) for _ in range(5)],
             pltpu.VMEM((steps, pairs - 1, blocks, scen, width), BF16),
-            pltpu.VMEM(mshape, BF16),
+            pltpu.VMEM((steps, pairs, rows, scen, width), BF16),
             pltpu.VMEM((steps, nu, rows, scen, width), F32),
             pltpu.VMEM((scen * count, width), F32),
             pltpu.VMEM((blocks * scen, width), F32),
             pltpu.VMEM((steps, 3, rows, scen, width), BF16),
             pltpu.VMEM((steps, 3, rows, scen, width), BF16),
+            pltpu.VMEM(panel, F32),
+            pltpu.VMEM(panel, BF16),
+            pltpu.VMEM(panel, BF16),
+            pltpu.VMEM(panel, BF16),
+            pltpu.VMEM((steps, 3, nu, scen, width), F32),
+            pltpu.VMEM((3, steps, scen, width), F32),
+            pltpu.VMEM((steps * pairs * scen, width), F32),
+            pltpu.VMEM((2, width, width), F32),
+            pltpu.VMEM((rows, width // 2, width), BF16),
+            pltpu.VMEM((rows, width // 2, width), BF16),
+            pltpu.VMEM((rows, nu, span // 2, width), BF16),
+            pltpu.VMEM((rows, nu, span // 2, width), BF16),
             dma((steps, 3)), dma((steps, 3)),
             dma((steps, 3, 2)), dma((steps, 3, 2)),
             dma((steps, 3, 2)), dma((steps, 3, 2)),
             dma((steps, 3)), dma((steps, 3)),
             dma((steps, 3)), dma((steps, 3)),
-            dma((steps + 1, 4)),
+            dma((steps, 3)), dma((steps, 3)),
+            dma((3,)), dma((3,)),
+            dma((2,)), dma((2,)),
+            dma((groups,)), dma((groups,)),
+            dma((groups,)), dma((groups,)),
         ],
         compiler_params=pltpu.CompilerParams(
             collective_id=0, has_side_effects=True, vmem_limit_bytes=60 * 2**20
         ),
         name="sweep",
-    )(drift_cols, control_cols, drift_blocks, control_blocks, wts, first, nxt, tgt, hits)
-
-    prev_end = passed_along(last, "tm", 1)
-    prev_defect = jnp.where(group_index > 0, first.astype(F32) - prev_end.astype(F32), 0.0)
-    grad_shooting = jnp.swapaxes(lam + defect_weight * prev_defect, 0, 1).reshape(1, scen, local)
+    )(drift_cols, control_cols, drift_blocks, control_blocks, wts, wex, first, tgt, hits)
+
+    grad_shooting = jnp.swapaxes(gshoot, 0, 1).reshape(1, scen, local)
     input_grads = jnp.swapaxes(jnp.sum(ig, -1), 0, 1)
-    grad_controls = lax.psum(input_grads, "rows") * (local * row_count) ** (-0.5)
-    grad_scale = (scen * steps * group_count) ** (-0.5)
-
-    groups = [[i for i in range(group_count) if i % 2 == b] for b in range(2)]
-    inputs = lax.all_gather(controls, "tm", axis_index_groups=groups)
-    span = width // slots
-    depth = steps * pairs * scen
-    cut = lax.dynamic_slice_in_dim(muall, pair * span, span, 4).astype(F32)
-    inputs = inputs.transpose(2, 0, 3, 1)[:, :, None, :, :, None]
-    weighted = (cut[:, :, :, :, None, :] * inputs).astype(BF16)
-    weighted = weighted.transpose(2, 4, 5, 0, 1, 3).reshape(rows, width, depth)
-    mu_t = muall.transpose(2, 4, 0, 1, 3).reshape(rows, width, depth)
-    dcol = lax.dynamic_index_in_dim(drift_cols, pair, 1, keepdims=False)
-    drift_sum, control_sum = pl.pallas_call(
-        sums_kernel,
-        out_shape=(
-            jax.ShapeDtypeStruct((rows, width, width), F32),
-            jax.ShapeDtypeStruct((nu, rows, span, width), F32),
-        ),
-        grid_spec=pltpu.PrefetchScalarGridSpec(
-            num_scalar_prefetch=2,
-            grid=(rows,),
-            in_specs=[
-                pl.BlockSpec(zshape, lambda i, *_: (0, 0, 0, 0, 0), pipeline_mode=pl.Buffered(1)),
-                pl.BlockSpec((1, width, depth), lambda i, *_: (i, 0, 0)),
-                pl.BlockSpec((1, width, depth), lambda i, *_: (i, 0, 0)),
-            ],
-            out_specs=[
-                pl.BlockSpec((1, width, width), lambda i, *_: (i, 0, 0)),
-                pl.BlockSpec((nu, 1, span, width), lambda i, *_: (0, i, 0, 0)),
-            ],
-        ),
-        name="sums",
-    )(dcol, control_cols, zall, mu_t, weighted)
-    drift_two = drift_sum.reshape(rows, 2, -1)
-    control_two = control_sum.reshape(nu, rows, 2, -1)
-    swap = [(i, i ^ 1) for i in range(group_count)]
-
-    def merged(two, axis):
-        mine = lax.dynamic_index_in_dim(two, half, axis, keepdims=False)
-        other = lax.dynamic_index_in_dim(two, 1 - half, axis, keepdims=False)
-        got = lax.ppermute(other.astype(BF16), "tm", swap)
-        return (mine + got.astype(F32)) * grad_scale
-
-    return (grad_shooting, grad_controls, merged(drift_two, 1), merged(control_two, 2))
+    grad_controls = input_grads * (local * row_count) ** (-0.5)
+    return (
+        grad_shooting,
+        grad_controls,
+        gdrift.reshape(rows, -1),
+        gcontrol.reshape(nu, rows, -1),
+    )
 
 
 def solution(mesh):

time: 221 us -> 146 us (0.66)
  local copies, waits for them, and re-layouts: 41.3 us -> 10.6 us
  blocking collectives: 27.9 us -> 0 us
  other arithmetic: 10.9 us -> 2.28 us
  waiting for transfers between devices: 7.54 us -> 0 us
  Pallas kernels: 125 us -> 132 us
  starting transfers between devices: 5.86 us -> 0 us
    mul x8 -> x0, local copies, waits for them, and re-layouts: 18.1 us -> none  [shards(): weighted = (cut[:, :, :, :, None, :] * inputs).astype(BF16)]
    all_gather x1 -> x0, blocking collectives: 16.8 us -> none  [shards(): inputs = lax.all_gather(controls, 'tm', axis_index_groups=groups)]
    psum x1 -> x0, blocking collectives: 11 us -> none  [shards(): lax.psum(input_grads, 'rows') * (local * row_count) ** (-0.5)]
    ppermute x4 -> x0, waiting for transfers between devices: 7.54 us -> none  [the longest x2 7.54 us: passed_along(): return lax.ppermute(value, axis, pairs)]
    pallas_call x2 -> x1, Pallas kernels: 125 us -> 132 us  [shards(): pl.pallas_call(sweep_kernel, out_shape=(jax.ShapeDtypeStruct(panel, F32),...]
    dynamic_slice x4 -> x0, local copies, waits for them, and re-layouts: 6.35 us -> none  [the longest x2 4.14 us: merged(): mine = lax.dynamic_index_in_dim(two, half, axis, keepdims=False)]
    ppermute x4 -> x0, starting transfers between devices: 5.86 us -> none  [the longest x2 3.83 us: passed_along(): return lax.ppermute(value, axis, pairs)]
    mul x4 -> x1, other arithmetic: 5.49 us -> 0.61 us  [shards(): grad_controls = input_grads * (local * row_count) ** (-0.5)]
  transfers between devices with their start and end apart: 4 -> 0, of which waited for: 1 -> 0; matrix products, arithmetic and copies ran while one was open for 4% -> 0% of each run, Pallas kernels for 0% -> 0%
where the time goes in v2:
time: 146 us
  Pallas kernels  132 us (90%)
  local copies, waits for them, and re-layouts  10.6 us (7%)
  other arithmetic  2.28 us (2%)
    pallas_call x1, Pallas kernels, shards(): pl.pallas_call(sweep_kernel, out_shape=(jax.ShapeDtypeStruct(panel, F32),...  132 us
    unnamed x7, local copies, waits for them, and re-layouts  4.23 us

profile of v2, /device:TPU:0, one launch (start us, length us, event | category | flops | bytes accessed | tf_op | source)
XLA Modules:
  0.0 145.6 jit_solution(13961024816826327606)
XLA Ops:
  0.6 0.8 copy.18.dcol
  1.4 0.0 copy-start
  1.4 0.1 reshape.33
  1.5 0.8 copy.17
  2.3 0.1 reshape.34
  2.4 0.8 copy.15
  3.2 0.1 broadcast_in_dim.5
  3.3 0.7 reshape.31.wex
  4.0 0.6 fusion.hits
  4.7 1.4 broadcast_in_dim.4.wts
  6.1 0.0 copy-done
  6.1 132.0 %sweep.1 = (f32[32,8,128]{2,1,0:T(8,128)}, f32[5,4,8,128]{3,2,1,0:T(8,128)}, f32[32,64,128]{2,1,0:T(8,128)}, f32[4,32,16,128]{3,2,1,0:T(8,128)}) custom-call(s32[32,4]{1,0:T(8,128)} %copy-done, s32[4,32]{1,0:T(4,128)} %ccol.1, bf16[32,4,128,128]{3,2,1,0:T(8,128)(2,1)} %drift.1, bf16[4,32,128,128]{3,2,1,0:T(8,128)(2,1)} %control.1, ...), custom_call_target="tpu_custom_call" | custom-call | tf_op jit(solution)/shard_map/sweep/pallas_call | solution.py:421
  138.1 0.0 copy-start.1
  138.1 1.0 reduce_sum.9
  139.1 0.6 multiply_bitcast_fusion
  139.7 2.8 %copy.21 = f32[4,8,64,128]{3,1,2,0:T(8,128)} copy(f32[4,8,64,128]{3,2,1,0:T(8,128)} %bitcast.21) | data formatting | bytes 2097152
  142.5 2.4 %reshape.37 = f32[4,32,2048]{2,1,0:T(8,128)} reshape(f32[4,32,16,128]{3,2,1,0:T(8,128)} %get-tuple-element.11) | data formatting | bytes 2097152 | tf_op jit(solution)/shard_map/reshape | solution.py:476
  144.9 0.0 copy-done.1
  144.9 0.7 copy.23
  (1 shorter events, 0.0 us)
Async XLA Ops:
  1.4 4.7 %copy-start = (s32[32,4]{1,0:T(8,128)}, s32[32,4]{1,0:T(8,128)S(1)}, u32[]{:S(2)}) copy-start(s32[32,4]{1,0:T(8,128)S(1)} %copy.18.dcol) | copy-start | bytes 1540
  138.1 6.8 %copy-start.1 = (f32[32,8,128]{2,1,0:T(8,128)S(1)}, f32[32,8,128]{2,1,0:T(8,128)}, u32[]{:S(2)}) copy-start(f32[32,8,128]{2,1,0:T(8,128)} %get-tuple-element.8) | copy-start | bytes 393220
